TPU v7x, 32 devices: a whole 2x2x4 slice. The times are simulated.
32 devices in a mesh: pp: 2 (over core), cp: 4 (over y, x), tp: 4 (over z).
Axes of the slice: x: 2, y: 2, z: 4, core: 2. Of those that a mesh axis runs over, the one named last changes fastest.
Arguments:
- query: bfloat16 [2, 512, 4096], P('pp', 'cp', 'tp'), may hold values from -120 to 120
- keyval: bfloat16 [2, 2, 512, 1024], P('pp', None, 'cp', 'tp'), may hold values from -4 to 4
- out_weight: bfloat16 [2, 4096, 4096], P('pp', None, 'tp'), may hold values from -0.375 to 0.375
- residual: bfloat16 [2, 512, 4096], P('pp', 'cp', 'tp'), may hold values from -3 to 3
- block_order: int32 [8], replicated, may hold values from 0 to 7, as said below
Outputs:
- handed: bfloat16 [2, 512, 4096], P('pp', 'cp', 'tp')
Inputs may be any that keep to these rules, and one draw needn't show every extreme that they name: A permutation of the 8 sequence blocks; context index c holds blocks block_order[2 c] and block_order[2 c + 1] in its first and second 64 rows.
All inputs are finite; a program needn't handle non-finite values.
Results may differ from a plain program's by a relative error of at most 0.013.
Values may be sent and summed in bfloat16 or wider, within the bound.
No kernel may reach another device: no remote copies, remote signals or barrier semaphores. Data moves between devices by JAX's collectives and lax.ppermute only.
A program may use at most 64 MiB of HBM per device.

v0:
```python
import math
import jax
import jax.numpy as jnp
from jax import lax
from jax.sharding import PartitionSpec as P

HD = 128
GROUP = 4
LOW_SCORE = -1e30


def shifted(value, axis, steps):
    count = lax.axis_size(axis)
    pairs = [(source, (source + steps) % count) for source in range(count)]
    return lax.ppermute(value, axis, pairs)


def positions(row_index, block_order, shard_rows, half_rows):
    slot_index = 2 * (row_index // shard_rows) + row_index % shard_rows // half_rows
    lookup = jnp.arange(block_order.shape[0], dtype=jnp.int32)
    picked = jnp.sum(
        jnp.where(slot_index[:, None] == lookup[None, :], block_order[None, :], 0), axis=1
    )
    return picked * half_rows + row_index % half_rows


def attend_piece(carried, queries, query_pos, key_rows, values, key_pos):
    weighted, row_peak, row_mass = carried
    scores = jnp.einsum("qkgd,nkd->qkgn", queries, key_rows, preferred_element_type=jnp.float32) * (
        1.0 / math.sqrt(HD)
    )
    visible = (key_pos[None, :] <= query_pos[:, None])[:, None, None, :]
    scores = jnp.where(visible, scores, LOW_SCORE)
    new_peak = jnp.maximum(row_peak, jnp.max(scores, axis=3))
    factor = jnp.exp(row_peak - new_peak)
    weights = jnp.where(visible, jnp.exp(scores - new_peak[..., None]), 0.0)
    rounded = weights.astype(jnp.bfloat16)
    weighted = weighted * factor[..., None] + jnp.einsum(
        "qkgn,nkd->qkgd", rounded, values, preferred_element_type=jnp.float32
    )
    row_mass = row_mass * factor + jnp.sum(weights, axis=3)
    return (weighted, new_peak, row_mass)


def guarded(carried, queries, query_pos, key_rows, values, key_pos):
    return attend_piece(carried, queries, query_pos, key_rows, values, key_pos)


def fold_rows(carried, queries, query_pos, key_rows, values, key_pos):
    total = key_rows.shape[0]
    if total <= 512 or total % 512 != 0:
        return guarded(carried, queries, query_pos, key_rows, values, key_pos)
    count = total // 512
    stacked = (
        key_rows.reshape((count, 512) + key_rows.shape[1:]),
        values.reshape((count, 512) + values.shape[1:]),
        key_pos.reshape(count, 512),
    )

    def advance(inner, block_in):
        return (guarded(inner, queries, query_pos, block_in[0], block_in[1], block_in[2]), None)

    result, unused = lax.scan(advance, carried, stacked)
    return result


def start_state(shard_rows, kv_count):
    return (
        jnp.zeros((shard_rows, kv_count, GROUP, HD), jnp.float32),
        jnp.full((shard_rows, kv_count, GROUP), LOW_SCORE, jnp.float32),
        jnp.zeros((shard_rows, kv_count, GROUP), jnp.float32),
    )


def local(query, keyval, out_weight, residual, block_order):
    shard_rows = query.shape[1]
    half_rows = shard_rows // 2
    cp_index = lax.axis_index("cp")
    own_rows = cp_index * shard_rows + jnp.arange(shard_rows, dtype=jnp.int32)
    query_pos = positions(own_rows, block_order, shard_rows, half_rows)
    weight = out_weight[0]
    kv_count = keyval.shape[3] // HD
    queries = query[0].reshape(shard_rows, kv_count, GROUP, HD)
    block_in = lax.all_gather(keyval, "cp", axis=2, tiled=True)
    piece_rows = block_in.shape[2]
    row_index = jnp.arange(piece_rows, dtype=jnp.int32)
    key_pos = positions(row_index, block_order, shard_rows, half_rows)
    key_rows = block_in[0, 0].reshape(piece_rows, kv_count, HD)
    values = block_in[0, 1].reshape(piece_rows, kv_count, HD)
    weighted, row_peak, row_mass = fold_rows(
        start_state(shard_rows, kv_count), queries, query_pos, key_rows, values, key_pos
    )
    own_heads = (
        (weighted / row_mass[..., None])
        .reshape(shard_rows, kv_count * GROUP * HD)
        .astype(jnp.bfloat16)
    )
    attended = lax.all_gather(own_heads, "tp", axis=1, tiled=True)
    resid_rows = residual[0]
    mixed_sum = jnp.dot(attended, weight, preferred_element_type=jnp.float32)
    layer_out = (mixed_sum + resid_rows.astype(jnp.float32)).astype(jnp.bfloat16)[None]
    return shifted(layer_out, "pp", 1)


def solution(mesh):
    placed = (
        P("pp", "cp", "tp"),
        P("pp", None, "cp", "tp"),
        P("pp", None, "tp"),
        P("pp", "cp", "tp"),
        P(),
    )
    return jax.shard_map(
        local, mesh=mesh, in_specs=placed, out_specs=P("pp", "cp", "tp"), check_vma=False
    )
```

profile of v0, /device:TPU:0, one launch (start us, length us, event | category | flops | bytes accessed | tf_op | source)
XLA Modules:
  0.0 67.0 jit_solution(8327772678584267992)
XLA Ops:
  6.5 0.0 all-gather.2.cloned.1.call-start
  6.6 0.7 %select_reduce_fusion.1 = s32[128]{0:T(128)S(1)} fusion(s32[8]{0:T(128)} %param.9, s32[128]{0:T(128)S(1)} %fusion.40), kind=kLoop, calls=%fused_computation.24 | loop fusion | flops 2944 | bytes 1056 | tf_op jit(solution)/shard_map/reduce_sum | solution.py:21
  7.3 0.7 %select_reduce_fusion = s32[512]{0:T(512)S(1)} fusion(s32[8]{0:T(128)} %param.9, s32[512]{0:T(512)S(1)} %fusion.29), kind=kLoop, calls=%fused_computation.21 | loop fusion | flops 11776 | bytes 4128 | tf_op jit(solution)/shard_map/reduce_sum | solution.py:21
  8.1 1.0 %copy.13 = bf16[1,2,128,256]{2,3,1,0:T(8,128)(2,1)S(1)} copy(bf16[1,2,128,256]{3,2,1,0:T(8,128)(2,1)} %param.6) | data formatting | bytes 262144 | tf_op args[1]
  9.1 1.1 %reshape_squeeze.10 = bf16[128,2,4,128]{3,2,1,0:T(4,128)(2,1)S(1)} reshape(bf16[1,128,1024]{2,1,0:T(8,128)(2,1)} %param.5) | data formatting | bytes 524288 | tf_op jit(solution)/shard_map/reshape;squeeze | solution.py:83
  10.2 11.5 %all_gather.6 = bf16[1,2,512,256]{2,3,1,0:T(8,128)(2,1)S(1)} all-gather(bf16[1,2,128,256]{2,3,1,0:T(8,128)(2,1)S(1)} %copy.13), channel_id=1, replica_groups=mesh['pp'=2,'cp'=4,'tp'=4] {'cp'}, dimensions={2}, use_global_device_ids=true | all-gather | bytes 655360 | tf_op jit(solution)/shard_map/all_gather | solution.py:84
  21.8 0.1 broadcast_compare_fusion
  21.9 0.5 fusion.2
  22.5 0.5 fusion.3
  23.0 0.0 copy-start
  23.0 1.4 %fusion.13 = bf16[128,2,4,128]{0,3,2,1:T(8,128)(2,1)} fusion(bf16[512,2,128,1]{0,2,3,1:T(8,128)(2,1)S(1)} %bitcast.49, f32[2,512,128,4]{2,1,3,0:T(8,128)S(1)} %get-tuple-element.10, f32[128,2,4]{0,2,1:T(4,128)S(1)} %broadcast_maximum_fusion, pred[128,512]{0,1:T(8,128)(4,1)S(1)} %broadcast_compare_fusion, f32[128,2,4]{0,2,1:T(4,128)S(1)} %get-tuple-element.8, ...), kind=kOutput, calls=%fused_computation.12 | convolution fusion | flops 137232384 | bytes 2699264 | tf_op jit(solution)/shard_map/qkgn,nkd->qkgd/dot_general | solution.py:38
  24.4 0.0 all-gather.2.cloned.1.call-update
  24.4 28.4 %all-gather.2.cloned.1.call-done = bf16[128,4096]{0,1:T(8,128)(2,1)} async-done(((bf16[128,1024]{0,1:T(8,128)(2,1)}), bf16[128,4096]{0,1:T(8,128)(2,1)}) %all-gather.2.cloned.1.call-update) | async-done | bytes 1048592 | tf_op jit(solution)/shard_map/all_gather | solution.py:98
  52.9 0.0 copy-done
  52.9 5.0 %fusion.14 = bf16[1,128,1024]{2,1,0:T(8,128)(2,1)S(1)} fusion(bf16[128,4096]{0,1:T(8,128)(2,1)} %all-gather.2.cloned.1.call-done, bf16[1,4096,1024]{2,1,0:T(8,128)(2,1)} %param.7, bf16[1,128,1024]{2,1,0:T(8,128)(2,1)S(1)} %copy-done), kind=kOutput, calls=%fused_computation.13 | convolution fusion | flops 1074135040 | bytes 9961472 | tf_op jit(solution)/shard_map/dot_general | solution.py:100
  57.9 0.1 collective-permute-start
  57.9 1.5 %collective-permute-done = bf16[1,128,1024]{2,1,0:T(8,128)(2,1)S(1)} collective-permute-done((bf16[1,128,1024]{2,1,0:T(8,128)(2,1)S(1)}, bf16[1,128,1024]{2,1,0:T(8,128)(2,1)S(1)}, u32[]{:S(2)}, u32[]{:S(2)}) %collective-permute-start) | collective-permute-done | bytes 262176 | tf_op jit(solution)/shard_map/ppermute | solution.py:15
  59.5 0.7 %copy.27 = bf16[1,128,1024]{2,1,0:T(8,128)(2,1)} copy(bf16[1,128,1024]{2,1,0:T(8,128)(2,1)S(1)} %collective-permute-done) | data formatting | bytes 524288
  (7 shorter events, 0.1 us)
Async XLA Ops:
  6.5 46.3 %all-gather.2.cloned.1.call-start = ((), (), s32[]{:S(2)}) async-start(), calls=%async_computation | async-start | bytes 1310720 | tf_op jit(solution)/shard_map/all_gather | solution.py:98
  23.0 29.8 %copy-start = (bf16[1,128,1024]{2,1,0:T(8,128)(2,1)S(1)}, bf16[1,128,1024]{2,1,0:T(8,128)(2,1)}, u32[]{:S(2)}) copy-start(bf16[1,128,1024]{2,1,0:T(8,128)(2,1)} %param.8) | copy-start | bytes 786436
  57.9 1.6 %collective-permute-start = (bf16[1,128,1024]{2,1,0:T(8,128)(2,1)S(1)}, bf16[1,128,1024]{2,1,0:T(8,128)(2,1)S(1)}, u32[]{:S(2)}, u32[]{:S(2)}) collective-permute-start(bf16[1,128,1024]{2,1,0:T(8,128)(2,1)S(1)} %fusion.14), channel_id=1, source_target_pairs={{0,16},{16,0},{1,17},{17,1},{2,18},{18,2},{3,19},{19,3},{4,20},{20... | collective-permute-start | bytes 786440 | tf_op jit(solution)/shard_map/ppermute | solution.py:15
Sparse Core Ops, SparseCore 0:
  24.6 28.2 all-gather.1
where the time goes:
time: 67.2 us; the launch traced here: 67 us
  waiting for transfers between devices  30 us (45%)
  between operations  13.5 us (20%)
  blocking collectives  11.5 us (17%)
  matrix products  6.91 us (10%)
  local copies, waits for them, and re-layouts  2.88 us (4%)
  other arithmetic  2.2 us (3%)
    all_gather x1, waiting for transfers between devices, local(): attended = lax.all_gather(own_heads, 'tp', axis=1, tiled=True)  28.4 us
    all_gather x1, blocking collectives, local(): block_in = lax.all_gather(keyval, 'cp', axis=2, tiled=True)  11.5 us
    dot_general x1, matrix products, local(): mixed_sum = jnp.dot(attended, weight, preferred_element_type=jnp.float32)  4.99 us
    unnamed x4, local copies, waits for them, and re-layouts  1.73 us
    ppermute x1, waiting for transfers between devices, shifted(): return lax.ppermute(value, axis, pairs)  1.52 us
    reduce_sum x2, other arithmetic, positions(): jnp.sum(jnp.where(slot_index[:, None] == lookup[None, :], block_order[Non...  1.48 us
    dot_general x1, matrix products, attend_piece(): jnp.einsum('qkgn,nkd->qkgd', rounded, values, preferred_element_type=jnp....  1.37 us
  transfers between devices with their start and end apart: 2, of which 2 were waited for; matrix products, arithmetic and copies ran while one was open for 0% of the time, Pallas kernels for 0%

commit v1 on v0

--- a/solution.py
+++ b/solution.py
@@ -81,7 +81,19 @@
     weight = out_weight[0]
     kv_count = keyval.shape[3] // HD
     queries = query[0].reshape(shard_rows, kv_count, GROUP, HD)
-    block_in = lax.all_gather(keyval, "cp", axis=2, tiled=True)
+    count_all = lax.axis_size("cp")
+    buffers = [keyval]
+    jj = 0
+    while jj < count_all - 1:
+        buffers.append(
+            lax.ppermute(
+                buffers[-1], "cp", perm=[(idx, (idx + 1) % count_all) for idx in range(count_all)]
+            )
+        )
+        jj += 1
+    block_in = jnp.roll(
+        jnp.concatenate(buffers[::-1], axis=2), (lax.axis_index("cp") + 1) * keyval.shape[2], axis=2
+    )
     piece_rows = block_in.shape[2]
     row_index = jnp.arange(piece_rows, dtype=jnp.int32)
     key_pos = positions(row_index, block_order, shard_rows, half_rows)

time: 67.2 us -> 72.7 us (1.082)
  waiting for transfers between devices: 30 us -> 42.8 us
  blocking collectives: 11.5 us -> 0 us
  starting transfers between devices: 0.07 us -> 3.88 us
    ppermute x0 -> x3, waiting for transfers between devices: none -> 12.6 us  [local(): lax.ppermute(buffers[-1], 'cp', perm=[(idx, (idx + 1) % count_all) for id...]
    all_gather x1 -> x0, blocking collectives: 11.5 us -> none  [local(): block_in = lax.all_gather(keyval, 'cp', axis=2, tiled=True)]
    ppermute x0 -> x3, starting transfers between devices: none -> 3.81 us  [local(): lax.ppermute(buffers[-1], 'cp', perm=[(idx, (idx + 1) % count_all) for id...]
    unnamed x4 -> x11, local copies, waits for them, and re-layouts: 1.73 us -> 1.99 us
  transfers between devices with their start and end apart: 2 -> 5, of which waited for: 2 -> 5; matrix products, arithmetic and copies ran while one was open for 0% -> 4% of each run, Pallas kernels for 0% -> 0%
where the time goes in v1:
time: 72.7 us; the launch traced here: 72.5 us
  waiting for transfers between devices  42.8 us (59%)
  between operations  13.5 us (19%)
  matrix products  6.92 us (10%)
  starting transfers between devices  3.88 us (5%)
  local copies, waits for them, and re-layouts  3.2 us (4%)
  other arithmetic  2.2 us (3%)
    all_gather x1, waiting for transfers between devices, local(): attended = lax.all_gather(own_heads, 'tp', axis=1, tiled=True)  28.7 us
    ppermute x3, waiting for transfers between devices, local(): lax.ppermute(buffers[-1], 'cp', perm=[(idx, (idx + 1) % count_all) for id...  12.6 us
    dot_general x1, matrix products, local(): mixed_sum = jnp.dot(attended, weight, preferred_element_type=jnp.float32)  5 us
    ppermute x3, starting transfers between devices, local(): lax.ppermute(buffers[-1], 'cp', perm=[(idx, (idx + 1) % count_all) for id...  3.81 us
    unnamed x11, local copies, waits for them, and re-layouts  1.99 us
    ppermute x1, waiting for transfers between devices, shifted(): return lax.ppermute(value, axis, pairs)  1.52 us
    reduce_sum x2, other arithmetic, positions(): jnp.sum(jnp.where(slot_index[:, None] == lookup[None, :], block_order[Non...  1.48 us
  transfers between devices with their start and end apart: 5, of which 5 were waited for; matrix products, arithmetic and copies ran while one was open for 4% of the time, Pallas kernels for 0%

profile of v1, /device:TPU:0, one launch (start us, length us, event | category | flops | bytes accessed | tf_op | source)
XLA Modules:
  0.0 72.5 jit_solution(2058970213779241515)
XLA Ops:
  6.5 0.0 all-gather.2.cloned.1.call-start
  6.5 1.0 %copy.15 = bf16[1,2,128,256]{2,3,1,0:T(8,128)(2,1)S(1)} copy(bf16[1,2,128,256]{3,2,1,0:T(8,128)(2,1)} %param.6) | data formatting | bytes 262144 | tf_op args[1]
  7.6 3.0 %collective-permute-start = (bf16[1,2,128,256]{2,3,1,0:T(8,128)(2,1)S(1)}, bf16[1,2,128,256]{2,3,1,0:T(8,128)(2,1)S(1)}, u32[]{:S(2)}, u32[]{:S(2)}) collective-permute-start(bf16[1,2,128,256]{2,3,1,0:T(8,128)(2,1)S(1)} %copy.15), channel_id=1, source_target_pairs={{0,4},{4,8},{8,12},{12,0},{1,5},{5,9},{9,13},{13,1},{2,6},{6,10},{... | collective-permute-start | bytes 393224 | tf_op jit(solution)/shard_map/ppermute | solution.py:89
  10.6 0.7 %select_reduce_fusion = s32[512]{0:T(512)S(1)} fusion(s32[8]{0:T(128)} %param.9, s32[512]{0:T(512)S(1)} %fusion.29), kind=kLoop, calls=%fused_computation.29 | loop fusion | flops 11776 | bytes 4128 | tf_op jit(solution)/shard_map/reduce_sum | solution.py:21
  11.4 1.1 %reshape_squeeze.10 = bf16[128,2,4,128]{3,2,1,0:T(4,128)(2,1)S(1)} reshape(bf16[1,128,1024]{2,1,0:T(8,128)(2,1)} %param.5) | data formatting | bytes 524288 | tf_op jit(solution)/shard_map/reshape;squeeze | solution.py:83
  12.5 0.7 %select_reduce_fusion.1 = s32[128]{0:T(128)S(1)} fusion(s32[8]{0:T(128)} %param.9, s32[128]{0:T(128)S(1)} %fusion.40), kind=kLoop, calls=%fused_computation.32 | loop fusion | flops 2944 | bytes 1056 | tf_op jit(solution)/shard_map/reduce_sum | solution.py:21
  13.2 1.8 %collective-permute-done = bf16[1,2,128,256]{2,3,1,0:T(8,128)(2,1)S(1)} collective-permute-done((bf16[1,2,128,256]{2,3,1,0:T(8,128)(2,1)S(1)}, bf16[1,2,128,256]{2,3,1,0:T(8,128)(2,1)S(1)}, u32[]{:S(2)}, u32[]{:S(2)}) %collective-permute-start) | collective-permute-done | bytes 131104 | tf_op jit(solution)/shard_map/ppermute | solution.py:89
  15.0 0.8 %collective-permute-start.1 = (bf16[1,2,128,256]{2,3,1,0:T(8,128)(2,1)S(1)}, bf16[1,2,128,256]{2,3,1,0:T(8,128)(2,1)S(1)}, u32[]{:S(2)}, u32[]{:S(2)}) collective-permute-start(bf16[1,2,128,256]{2,3,1,0:T(8,128)(2,1)S(1)} %collective-permute-done), channel_id=1, source_target_pairs={{0,4},{4,8},{8,12},{12,0},{1,5},{5,9},{9,13},{13,1},{2,6},{6,10},{... | collective-permute-start | bytes 393224 | tf_op jit(solution)/shard_map/ppermute | solution.py:89
  15.8 5.1 %collective-permute-done.1 = bf16[1,2,128,256]{2,3,1,0:T(8,128)(2,1)S(1)} collective-permute-done((bf16[1,2,128,256]{2,3,1,0:T(8,128)(2,1)S(1)}, bf16[1,2,128,256]{2,3,1,0:T(8,128)(2,1)S(1)}, u32[]{:S(2)}, u32[]{:S(2)}) %collective-permute-start.1) | collective-permute-done | bytes 131104 | tf_op jit(solution)/shard_map/ppermute | solution.py:89
  20.9 0.0 collective-permute-start.2
  20.9 0.1 broadcast_compare_fusion
  21.0 5.7 %collective-permute-done.2 = bf16[1,2,128,256]{2,3,1,0:T(8,128)(2,1)S(1)} collective-permute-done((bf16[1,2,128,256]{2,3,1,0:T(8,128)(2,1)S(1)}, bf16[1,2,128,256]{2,3,1,0:T(8,128)(2,1)S(1)}, u32[]{:S(2)}, u32[]{:S(2)}) %collective-permute-start.2) | collective-permute-done | bytes 131104 | tf_op jit(solution)/shard_map/ppermute | solution.py:89
  27.2 0.5 fusion.2
  27.7 0.5 fusion.3
  28.3 0.0 copy-start
  28.3 1.4 %fusion.13 = bf16[128,2,4,128]{0,3,2,1:T(8,128)(2,1)} fusion(bf16[512,2,128,1]{0,2,3,1:T(8,128)(2,1)S(1)} %bitcast.48, f32[2,512,128,4]{2,1,3,0:T(8,128)S(1)} %get-tuple-element.10, f32[128,2,4]{0,2,1:T(4,128)S(1)} %broadcast_maximum_fusion, pred[128,512]{0,1:T(8,128)(4,1)S(1)} %broadcast_compare_fusion, f32[128,2,4]{0,2,1:T(4,128)S(1)} %get-tuple-element.8, ...), kind=kOutput, calls=%fused_computation.12 | convolution fusion | flops 137232384 | bytes 2699264 | tf_op jit(solution)/shard_map/qkgn,nkd->qkgd/dot_general | solution.py:38
  29.7 0.0 all-gather.2.cloned.1.call-update
  29.7 28.7 %all-gather.2.cloned.1.call-done = bf16[128,4096]{0,1:T(8,128)(2,1)} async-done(((bf16[128,1024]{0,1:T(8,128)(2,1)}), bf16[128,4096]{0,1:T(8,128)(2,1)}) %all-gather.2.cloned.1.call-update) | async-done | bytes 1048592 | tf_op jit(solution)/shard_map/all_gather | solution.py:110
  58.3 0.0 copy-done
  58.3 5.0 %fusion.14 = bf16[1,128,1024]{2,1,0:T(8,128)(2,1)S(1)} fusion(bf16[128,4096]{0,1:T(8,128)(2,1)} %all-gather.2.cloned.1.call-done, bf16[1,4096,1024]{2,1,0:T(8,128)(2,1)} %param.7, bf16[1,128,1024]{2,1,0:T(8,128)(2,1)S(1)} %copy-done), kind=kOutput, calls=%fused_computation.13 | convolution fusion | flops 1074135040 | bytes 9961472 | tf_op jit(solution)/shard_map/dot_general | solution.py:112
  63.4 0.1 collective-permute-start.3
  63.4 1.5 %collective-permute-done.3 = bf16[1,128,1024]{2,1,0:T(8,128)(2,1)S(1)} collective-permute-done((bf16[1,128,1024]{2,1,0:T(8,128)(2,1)S(1)}, bf16[1,128,1024]{2,1,0:T(8,128)(2,1)S(1)}, u32[]{:S(2)}, u32[]{:S(2)}) %collective-permute-start.3) | collective-permute-done | bytes 262176 | tf_op jit(solution)/shard_map/ppermute | solution.py:15
  65.0 0.7 copy.38
  (15 shorter events, 0.4 us)
Async XLA Ops:
  6.5 51.8 %all-gather.2.cloned.1.call-start = ((), (), s32[]{:S(2)}) async-start(), calls=%async_computation | async-start | bytes 1310720 | tf_op jit(solution)/shard_map/all_gather | solution.py:110
  7.6 7.5 %collective-permute-start = (bf16[1,2,128,256]{2,3,1,0:T(8,128)(2,1)S(1)}, bf16[1,2,128,256]{2,3,1,0:T(8,128)(2,1)S(1)}, u32[]{:S(2)}, u32[]{:S(2)}) collective-permute-start(bf16[1,2,128,256]{2,3,1,0:T(8,128)(2,1)S(1)} %copy.15), channel_id=1, source_target_pairs={{0,4},{4,8},{8,12},{12,0},{1,5},{5,9},{9,13},{13,1},{2,6},{6,10},{... | collective-permute-start | bytes 393224 | tf_op jit(solution)/shard_map/ppermute | solution.py:89
  15.0 5.9 %collective-permute-start.1 = (bf16[1,2,128,256]{2,3,1,0:T(8,128)(2,1)S(1)}, bf16[1,2,128,256]{2,3,1,0:T(8,128)(2,1)S(1)}, u32[]{:S(2)}, u32[]{:S(2)}) collective-permute-start(bf16[1,2,128,256]{2,3,1,0:T(8,128)(2,1)S(1)} %collective-permute-done), channel_id=1, source_target_pairs={{0,4},{4,8},{8,12},{12,0},{1,5},{5,9},{9,13},{13,1},{2,6},{6,10},{... | collective-permute-start | bytes 393224 | tf_op jit(solution)/shard_map/ppermute | solution.py:89
  20.9 5.9 %collective-permute-start.2 = (bf16[1,2,128,256]{2,3,1,0:T(8,128)(2,1)S(1)}, bf16[1,2,128,256]{2,3,1,0:T(8,128)(2,1)S(1)}, u32[]{:S(2)}, u32[]{:S(2)}) collective-permute-start(bf16[1,2,128,256]{2,3,1,0:T(8,128)(2,1)S(1)} %collective-permute-done.1), channel_id=1, source_target_pairs={{0,4},{4,8},{8,12},{12,0},{1,5},{5,9},{9,13},{13,1},{2,6},{6,10},{... | collective-permute-start | bytes 393224 | tf_op jit(solution)/shard_map/ppermute | solution.py:89
  28.3 30.1 %copy-start = (bf16[1,128,1024]{2,1,0:T(8,128)(2,1)S(1)}, bf16[1,128,1024]{2,1,0:T(8,128)(2,1)}, u32[]{:S(2)}) copy-start(bf16[1,128,1024]{2,1,0:T(8,128)(2,1)} %param.8) | copy-start | bytes 786436
  63.4 1.6 %collective-permute-start.3 = (bf16[1,128,1024]{2,1,0:T(8,128)(2,1)S(1)}, bf16[1,128,1024]{2,1,0:T(8,128)(2,1)S(1)}, u32[]{:S(2)}, u32[]{:S(2)}) collective-permute-start(bf16[1,128,1024]{2,1,0:T(8,128)(2,1)S(1)} %fusion.14), channel_id=1, source_target_pairs={{0,16},{16,0},{1,17},{17,1},{2,18},{18,2},{3,19},{19,3},{4,20},{20... | collective-permute-start | bytes 786440 | tf_op jit(solution)/shard_map/ppermute | solution.py:15
Sparse Core Ops, SparseCore 0:
  29.8 28.4 all-gather.1
